TPU v7x, 32 devices: a whole 2x2x4 slice. The times are simulated.
32 devices in a mesh: seqa: 4 (over x, core), seqb: 8 (over z, y).
Axes of the slice: x: 2, y: 2, z: 4, core: 2. Of those that a mesh axis runs over, the one named last changes fastest.
Arguments:
- sequence_input: bfloat16 [16384, 640], P(('seqa', 'seqb')), may hold values from -6 to 6
- w_prev: bfloat16 [3, 640, 1280], P(None, 'seqa'), may hold values from -0.15625 to 0.15625
- w_now: bfloat16 [3, 640, 1280], P(None, 'seqa'), may hold values from -0.15625 to 0.15625
- conv_bias: float32 [3, 1280], replicated, may hold values from -4 to 4
- w_mix: bfloat16 [3, 640, 640], P(None, None, 'seqa'), may hold values from -0.25 to 0.25
Outputs:
- seq_out: bfloat16 [16384, 640], P(('seqa', 'seqb'))
All inputs are finite; a program needn't handle non-finite values.
Results may differ from a plain program's by a relative error of at most 0.0052.
Values may be sent and summed in bfloat16 or wider, within the bound.
A program may use at most 64 MiB of HBM per device.

v0:
```python
import jax
import jax.numpy as jnp
from jax import lax
from jax.sharding import PartitionSpec as P

D = 640
DILATION_FIRST1 = 128
DILATION_SECOND2 = 512
DILATION_THIRD3 = 2048


def from_behind(value, axis, by):
    peers = lax.axis_size(axis)
    pairs = [(i, i + by) for i in range(peers) if 0 <= i + by < peers]
    return lax.ppermute(value, axis, pairs)


def norm_rows(values):
    scale = lax.rsqrt(jnp.mean(values * values, axis=1, keepdims=True) + 1e-06)
    return (values * scale).astype(jnp.bfloat16)


def block_prior(normed, dilation_step):
    rows = normed.shape[0]
    whole = dilation_step // rows
    part = dilation_step % rows
    pieces = []
    if part > 0:
        pieces.append(from_behind(normed[rows - part :], ("seqa", "seqb"), whole + 1))
    head = normed[: rows - part]
    if whole > 0:
        head = from_behind(head, ("seqa", "seqb"), whole)
    pieces.append(head)
    return jnp.concatenate(pieces, axis=0)


def one_layer(hidden_state, tap_prev, tap_now, bias, mixing, dilation_step):
    normed = norm_rows(hidden_state)
    earlier = block_prior(normed, dilation_step)
    rows = hidden_state.shape[0]
    start_sum = jnp.broadcast_to(bias[None, :], (rows, bias.shape[0]))
    total = start_sum
    total = total + jnp.dot(
        earlier,
        lax.all_gather(tap_prev, "seqa", axis=0, tiled=True),
        preferred_element_type=jnp.float32,
    )
    pre = total + jnp.dot(
        normed,
        lax.all_gather(tap_now, "seqa", axis=0, tiled=True),
        preferred_element_type=jnp.float32,
    )
    hidden = (pre[:, :D] * jax.nn.sigmoid(pre[:, D:])).astype(jnp.bfloat16)
    return hidden_state + jnp.dot(
        hidden,
        lax.all_gather(mixing, "seqa", axis=1, tiled=True),
        preferred_element_type=jnp.float32,
    )


def local(sequence_input, w_prev, w_now, conv_bias, w_mix):
    hidden_state = sequence_input.astype(jnp.float32)
    for layer_index, dilation_step in enumerate(
        (DILATION_FIRST1, DILATION_SECOND2, DILATION_THIRD3)
    ):
        hidden_state = one_layer(
            hidden_state,
            w_prev[layer_index],
            w_now[layer_index],
            conv_bias[layer_index],
            w_mix[layer_index],
            dilation_step,
        )
    block_output = hidden_state.astype(jnp.bfloat16)
    return block_output


def solution(mesh):
    return jax.shard_map(
        local,
        mesh=mesh,
        in_specs=(
            P(("seqa", "seqb"), None),
            P(None, "seqa", None),
            P(None, "seqa", None),
            P(),
            P(None, None, "seqa"),
        ),
        out_specs=P(("seqa", "seqb"), None),
        check_vma=False,
    )
```

profile of v0, /device:TPU:0, one launch (start us, length us, event | category | flops | bytes accessed | tf_op | source)
XLA Modules:
  0.0 173.4 jit_solution(16757699871526327815)
XLA Ops:
  6.5 2.4 %fusion.47 = (bf16[1,160,1280]{2,1,0:T(8,128)(2,1)}, bf16[1,160,1280]{2,1,0:T(8,128)(2,1)}, bf16[1,160,1280]{2,1,0:T(8,128)(2,1)}) fusion(bf16[3,160,1280]{2,1,0:T(8,128)(2,1)} %param.7), kind=kLoop, calls=%fused_computation.65 | loop fusion | bytes 2457600 | tf_op jit(solution)/shard_map/slice | solution.py:69
  9.0 0.0 all-gather.18.cloned.1.call-update
  9.0 0.0 all-gather.16.cloned.1.call-start
  9.1 1.1 fusion.46
  10.2 0.0 all-gather.16.cloned.1.call-update
  10.2 0.0 all-gather.22.cloned.1.call-start
  10.2 0.7 all-gather.22.cloned.1.call-update
  10.9 0.0 all-gather.20.cloned.1.call-start
  11.0 0.5 all-gather.20.cloned.1.call-update
  11.5 0.0 all-gather.26.cloned.1.call-start
  11.5 0.5 all-gather.26.cloned.1.call-update
  12.1 0.0 all-gather.24.cloned.1.call-start
  12.1 0.2 fusion.13
  12.4 0.0 copy-start.12
  12.4 0.0 copy-start.11
  12.4 0.2 fusion.14
  12.6 0.0 copy-start.1
  12.6 0.7 slice.80
  13.3 5.6 %collective-permute-start = (bf16[128,640]{1,0:T(8,128)(2,1)}, bf16[128,640]{1,0:T(8,128)(2,1)}, u32[]{:S(2)}, u32[]{:S(2)}) collective-permute-start(bf16[128,640]{1,0:T(8,128)(2,1)} %slice.80), channel_id=1, source_target_pairs={{0,1},{1,2},{2,3},{3,4},{4,5},{5,6},{6,7},{7,8},{8,9},{9,10},{10,1... | collective-permute-start | bytes 491528 | tf_op jit(solution)/shard_map/ppermute | solution.py:15
  18.9 0.0 all-gather.24.cloned.1.call-update
  18.9 0.9 slice.81
  19.8 0.7 fusion.48
  20.5 13.9 %all-gather.2 = bf16[1,640,640]{1,2,0:T(8,128)(2,1)} all-gather(bf16[1,640,160]{1,2,0:T(8,128)(2,1)S(1)} %get-tuple-element.15), channel_id=4, replica_groups=mesh['seqa'=4,'seqb'=8] {'seqa'}, dimensions={2}, use_global_device_ids=true | all-gather | bytes 1024000 | tf_op jit(solution)/shard_map/all_gather | solution.py:56
  34.4 1.9 %all-gather.18.cloned.1.call-done = bf16[1,640,1280]{2,1,0:T(8,128)(2,1)} async-done(((bf16[1,160,1280]{2,1,0:T(8,128)(2,1)}), bf16[1,640,1280]{2,1,0:T(8,128)(2,1)}) %all-gather.18.cloned.1.call-update) | async-done | bytes 1638416 | tf_op jit(solution)/shard_map/all_gather | solution.py:50
  36.3 2.8 %fusion.9 = f32[512,1280]{1,0:T(8,128)S(1)} fusion(bf16[512,640]{1,0:T(8,128)(2,1)} %copy-done.1, bf16[1,640,1280]{2,1,0:T(8,128)(2,1)} %all-gather.18.cloned.1.call-done), kind=kOutput, calls=%fused_computation.15 | convolution fusion | flops 838860800 | bytes 4915200 | tf_op jit(solution)/shard_map/dot_general | solution.py:48
  39.1 0.0 collective-permute-done
  39.1 18.8 %all-gather.16.cloned.1.call-done = bf16[1,640,1280]{2,1,0:T(8,128)(2,1)} async-done(((bf16[1,160,1280]{2,1,0:T(8,128)(2,1)}), bf16[1,640,1280]{2,1,0:T(8,128)(2,1)}) %all-gather.16.cloned.1.call-update) | async-done | bytes 1638416 | tf_op jit(solution)/shard_map/all_gather | solution.py:45
  57.9 2.9 %fusion = f32[512,1280]{1,0:T(8,128)S(1)} fusion(f32[512,1280]{1,0:T(8,128)S(1)} %fusion.9, bf16[1,640,1280]{2,1,0:T(8,128)(2,1)} %all-gather.16.cloned.1.call-done, f32[1280]{0:T(1024)S(1)} %get-tuple-element.6, bf16[384,640]{1,0:T(8,128)(2,1)} %slice.81, bf16[128,640]{1,0:T(8,128)(2,1)} %collective-permute-done), kind=kOutput, calls=%fused_computation.3 | convolution fusion | flops 841482240 | bytes 7541760 | tf_op jit(solution)/shard_map/dot_general | solution.py:43
  60.8 1.0 multiply_reduce_fusion.1
  61.8 1.0 copy-done.4
  62.9 1.0 multiply_convert_fusion.1
  63.8 4.3 %collective-permute-start.1 = (bf16[512,640]{1,0:T(8,128)(2,1)}, bf16[512,640]{1,0:T(8,128)(2,1)}, u32[]{:S(2)}, u32[]{:S(2)}) collective-permute-start(bf16[512,640]{1,0:T(8,128)(2,1)} %multiply_convert_fusion.1), channel_id=1, source_target_pairs={{0,1},{1,2},{2,3},{3,4},{4,5},{5,6},{6,7},{7,8},{8,9},{9,10},{10,1... | collective-permute-start | bytes 1966088 | tf_op jit(solution)/shard_map/ppermute | solution.py:15
  68.1 13.7 %all-gather.5 = bf16[1,640,640]{1,2,0:T(8,128)(2,1)} all-gather(bf16[1,640,160]{1,2,0:T(8,128)(2,1)S(1)} %copy-done.7), channel_id=7, replica_groups=mesh['seqa'=4,'seqb'=8] {'seqa'}, dimensions={2}, use_global_device_ids=true | all-gather | bytes 1024000 | tf_op jit(solution)/shard_map/all_gather | solution.py:56
  81.8 2.1 %all-gather.22.cloned.1.call-done = bf16[1,640,1280]{2,1,0:T(8,128)(2,1)} async-done(((bf16[1,160,1280]{2,1,0:T(8,128)(2,1)}), bf16[1,640,1280]{2,1,0:T(8,128)(2,1)}) %all-gather.22.cloned.1.call-update) | async-done | bytes 1638416 | tf_op jit(solution)/shard_map/all_gather | solution.py:50
  83.9 2.8 %fusion.6 = f32[512,1280]{1,0:T(8,128)S(1)} fusion(bf16[512,640]{1,0:T(8,128)(2,1)} %multiply_convert_fusion.1, bf16[1,640,1280]{2,1,0:T(8,128)(2,1)} %all-gather.22.cloned.1.call-done), kind=kOutput, calls=%fused_computation.12 | convolution fusion | flops 838860800 | bytes 4915200 | tf_op jit(solution)/shard_map/dot_general | solution.py:48
  86.7 22.9 %all-gather.20.cloned.1.call-done = bf16[1,640,1280]{2,1,0:T(8,128)(2,1)} async-done(((bf16[1,160,1280]{2,1,0:T(8,128)(2,1)}), bf16[1,640,1280]{2,1,0:T(8,128)(2,1)}) %all-gather.20.cloned.1.call-update) | async-done | bytes 1638416 | tf_op jit(solution)/shard_map/all_gather | solution.py:45
  109.6 3.0 %fusion.1 = f32[512,1280]{1,0:T(8,128)S(1)} fusion(f32[512,1280]{1,0:T(8,128)S(1)} %fusion.6, bf16[512,640]{1,0:T(8,128)(2,1)} %collective-permute-done.1, bf16[1,640,1280]{2,1,0:T(8,128)(2,1)} %all-gather.20.cloned.1.call-done, f32[1280]{0:T(1024)S(1)} %get-tuple-element.7), kind=kOutput, calls=%fused_computation.4 | convolution fusion | flops 840171520 | bytes 7541760 | tf_op jit(solution)/shard_map/dot_general | solution.py:43
  112.6 1.0 multiply_reduce_fusion
  113.6 1.1 copy-done.2
  114.6 1.0 multiply_convert_fusion
  115.6 4.3 %collective-permute-start.2 = (bf16[512,640]{1,0:T(8,128)(2,1)}, bf16[512,640]{1,0:T(8,128)(2,1)S(1)}, u32[]{:S(2)}, u32[]{:S(2)}) collective-permute-start(bf16[512,640]{1,0:T(8,128)(2,1)} %multiply_convert_fusion), channel_id=1, source_target_pairs={{0,4},{1,5},{2,6},{3,7},{4,8},{5,9},{6,10},{7,11},{8,12},{9,13},{1... | collective-permute-start | bytes 1966088 | tf_op jit(solution)/shard_map/ppermute | solution.py:15
  120.0 14.0 %all-gather.8 = bf16[1,640,640]{1,2,0:T(8,128)(2,1)} all-gather(bf16[1,640,160]{1,2,0:T(8,128)(2,1)S(1)} %get-tuple-element.14), channel_id=10, replica_groups=mesh['seqa'=4,'seqb'=8] {'seqa'}, dimensions={2}, use_global_device_ids=true | all-gather | bytes 1024000 | tf_op jit(solution)/shard_map/all_gather | solution.py:56
  134.0 1.4 all-gather.26.cloned.1.call-done
  135.4 2.8 %fusion.3 = f32[512,1280]{1,0:T(8,128)S(1)} fusion(bf16[512,640]{1,0:T(8,128)(2,1)} %multiply_convert_fusion, bf16[1,640,1280]{2,1,0:T(8,128)(2,1)} %all-gather.26.cloned.1.call-done), kind=kOutput, calls=%fused_computation.9 | convolution fusion | flops 838860800 | bytes 4915200 | tf_op jit(solution)/shard_map/dot_general | solution.py:48
  138.2 23.8 %all-gather.24.cloned.1.call-done = bf16[1,640,1280]{2,1,0:T(8,128)(2,1)} async-done(((bf16[1,160,1280]{2,1,0:T(8,128)(2,1)}), bf16[1,640,1280]{2,1,0:T(8,128)(2,1)}) %all-gather.24.cloned.1.call-update) | async-done | bytes 1638416 | tf_op jit(solution)/shard_map/all_gather | solution.py:45
  162.0 0.0 collective-permute-done.2
  162.0 2.8 %fusion.2 = f32[512,1280]{1,0:T(8,128)S(1)} fusion(f32[512,1280]{1,0:T(8,128)S(1)} %fusion.3, bf16[512,640]{1,0:T(8,128)(2,1)S(1)} %collective-permute-done.2, bf16[1,640,1280]{2,1,0:T(8,128)(2,1)} %all-gather.24.cloned.1.call-done, f32[1280]{0:T(1024)S(1)} %get-tuple-element.5), kind=kOutput, calls=%fused_computation.5 | convolution fusion | flops 840171520 | bytes 7541760 | tf_op jit(solution)/shard_map/dot_general | solution.py:43
  164.8 1.7 fusion.12
  (27 shorter events, 0.1 us)
Async XLA Ops:
  6.5 2.5 %copy-start.6 = (bf16[3,160,1280]{2,1,0:T(8,128)(2,1)S(1)}, bf16[3,160,1280]{2,1,0:T(8,128)(2,1)}, u32[]{:S(2)}) copy-start(bf16[3,160,1280]{2,1,0:T(8,128)(2,1)} %param.6) | copy-start | bytes 3686404
  6.5 29.7 %all-gather.18.cloned.1.call-start = ((), (), s32[]{:S(2)}) async-start(), calls=%async_computation.1 | async-start | bytes 2048000 | tf_op jit(solution)/shard_map/all_gather | solution.py:50
  9.0 48.9 %all-gather.16.cloned.1.call-start = ((), (), s32[]{:S(2)}) async-start(), calls=%async_computation | async-start | bytes 2048000 | tf_op jit(solution)/shard_map/all_gather | solution.py:45
  10.2 2.0 %copy-start = (bf16[512,640]{1,0:T(8,128)(2,1)S(1)}, bf16[512,640]{1,0:T(8,128)(2,1)}, u32[]{:S(2)}) copy-start(bf16[512,640]{1,0:T(8,128)(2,1)} %param.5) | copy-start | bytes 1966084
  10.2 73.7 %all-gather.22.cloned.1.call-start = ((), (), s32[]{:S(2)}) async-start(), calls=%async_computation.3 | async-start | bytes 2048000 | tf_op jit(solution)/shard_map/all_gather | solution.py:50
  10.9 98.6 %all-gather.20.cloned.1.call-start = ((), (), s32[]{:S(2)}) async-start(), calls=%async_computation.2 | async-start | bytes 2048000 | tf_op jit(solution)/shard_map/all_gather | solution.py:45
  11.5 123.9 %all-gather.26.cloned.1.call-start = ((), (), s32[]{:S(2)}) async-start(), calls=%async_computation.5 | async-start | bytes 2048000 | tf_op jit(solution)/shard_map/all_gather | solution.py:50
  12.1 149.9 %all-gather.24.cloned.1.call-start = ((), (), s32[]{:S(2)}) async-start(), calls=%async_computation.4 | async-start | bytes 2048000 | tf_op jit(solution)/shard_map/all_gather | solution.py:45
  12.4 7.4 %copy-start.12 = (f32[3,1280]{1,0:T(4,128)S(1)}, f32[3,1280]{1,0:T(4,128)}, u32[]{:S(2)}) copy-start(f32[3,1280]{1,0:T(4,128)} %param.8) | copy-start | bytes 46084
  12.4 7.4 %copy-start.11 = (bf16[3,640,160]{1,2,0:T(8,128)(2,1)S(1)}, bf16[3,640,160]{1,2,0:T(8,128)(2,1)}, u32[]{:S(2)}) copy-start(bf16[3,640,160]{1,2,0:T(8,128)(2,1)} %param.9) | copy-start | bytes 1843204
  12.6 8.0 %copy-start.1 = (bf16[512,640]{1,0:T(8,128)(2,1)}, bf16[512,640]{1,0:T(8,128)(2,1)S(1)}, u32[]{:S(2)}) copy-start(bf16[512,640]{1,0:T(8,128)(2,1)S(1)} %fusion.14) | copy-start | bytes 1966084
  13.3 25.8 %collective-permute-start = (bf16[128,640]{1,0:T(8,128)(2,1)}, bf16[128,640]{1,0:T(8,128)(2,1)}, u32[]{:S(2)}, u32[]{:S(2)}) collective-permute-start(bf16[128,640]{1,0:T(8,128)(2,1)} %slice.80), channel_id=1, source_target_pairs={{0,1},{1,2},{2,3},{3,4},{4,5},{5,6},{6,7},{7,8},{8,9},{9,10},{10,1... | collective-permute-start | bytes 491528 | tf_op jit(solution)/shard_map/ppermute | solution.py:15
  57.9 2.9 %copy-start.8 = (bf16[1,640,640]{1,2,0:T(8,128)(2,1)S(1)}, bf16[1,640,640]{1,2,0:T(8,128)(2,1)}, u32[]{:S(2)}) copy-start(bf16[1,640,640]{1,2,0:T(8,128)(2,1)} %all-gather.2) | copy-start | bytes 2457604
  61.8 1.1 copy-start.4
  61.8 6.3 %copy-start.7 = (bf16[1,640,160]{1,2,0:T(8,128)(2,1)S(1)}, bf16[1,640,160]{1,2,0:T(8,128)(2,1)}, u32[]{:S(2)}) copy-start(bf16[1,640,160]{1,2,0:T(8,128)(2,1)} %get-tuple-element.16) | copy-start | bytes 614404
  63.8 45.7 %collective-permute-start.1 = (bf16[512,640]{1,0:T(8,128)(2,1)}, bf16[512,640]{1,0:T(8,128)(2,1)}, u32[]{:S(2)}, u32[]{:S(2)}) collective-permute-start(bf16[512,640]{1,0:T(8,128)(2,1)} %multiply_convert_fusion.1), channel_id=1, source_target_pairs={{0,1},{1,2},{2,3},{3,4},{4,5},{5,6},{6,7},{7,8},{8,9},{9,10},{10,1... | collective-permute-start | bytes 1966088 | tf_op jit(solution)/shard_map/ppermute | solution.py:15
  109.6 3.0 %copy-start.5 = (f32[512,640]{1,0:T(8,128)S(1)}, f32[512,640]{1,0:T(8,128)}, u32[]{:S(2)}) copy-start(f32[512,640]{1,0:T(8,128)} %copy-done.4) | copy-start | bytes 3932164
  109.6 3.0 %copy-start.9 = (bf16[1,640,640]{1,2,0:T(8,128)(2,1)S(1)}, bf16[1,640,640]{1,2,0:T(8,128)(2,1)}, u32[]{:S(2)}) copy-start(bf16[1,640,640]{1,2,0:T(8,128)(2,1)} %all-gather.5) | copy-start | bytes 2457604
  113.5 1.1 copy-start.2
  115.6 46.4 %collective-permute-start.2 = (bf16[512,640]{1,0:T(8,128)(2,1)}, bf16[512,640]{1,0:T(8,128)(2,1)S(1)}, u32[]{:S(2)}, u32[]{:S(2)}) collective-permute-start(bf16[512,640]{1,0:T(8,128)(2,1)} %multiply_convert_fusion), channel_id=1, source_target_pairs={{0,4},{1,5},{2,6},{3,7},{4,8},{5,9},{6,10},{7,11},{8,12},{9,13},{1... | collective-permute-start | bytes 1966088 | tf_op jit(solution)/shard_map/ppermute | solution.py:15
  162.0 2.8 %copy-start.3 = (f32[512,640]{1,0:T(8,128)S(1)}, f32[512,640]{1,0:T(8,128)}, u32[]{:S(2)}) copy-start(f32[512,640]{1,0:T(8,128)} %copy-done.2) | copy-start | bytes 3932164
  162.0 2.8 %copy-start.10 = (bf16[1,640,640]{1,2,0:T(8,128)(2,1)S(1)}, bf16[1,640,640]{1,2,0:T(8,128)(2,1)}, u32[]{:S(2)}) copy-start(bf16[1,640,640]{1,2,0:T(8,128)(2,1)} %all-gather.8) | copy-start | bytes 2457604
Sparse Core Ops, SparseCore 0:
  9.1 27.0 all-gather.17
  37.8 19.9 all-gather.15
  59.4 24.3 all-gather.21
  85.3 24.2 all-gather.19
  111.0 24.3 all-gather.25
  136.8 25.1 all-gather.23
where the time goes:
time: 174 us; the launch traced here: 173 us
  waiting for transfers between devices  72.5 us (42%)
  blocking collectives  41.6 us (24%)
  matrix products  20.8 us (12%)
  starting transfers between devices  14.4 us (8%)
  between operations  13.7 us (8%)
  local copies, waits for them, and re-layouts  8.03 us (5%)
  other arithmetic  2.36 us (1%)
    all_gather x3, waiting for transfers between devices, one_layer(): lax.all_gather(tap_prev, 'seqa', axis=0, tiled=True)  65.4 us
    all_gather x3, blocking collectives, one_layer(): lax.all_gather(mixing, 'seqa', axis=1, tiled=True)  41.6 us
    ppermute x3, starting transfers between devices, from_behind(): return lax.ppermute(value, axis, pairs)  14.2 us
    dot_general x3, matrix products, one_layer(): jnp.dot(earlier, lax.all_gather(tap_prev, 'seqa', axis=0, tiled=True), pr...  8.68 us
    dot_general x3, matrix products, one_layer(): jnp.dot(normed, lax.all_gather(tap_now, 'seqa', axis=0, tiled=True), pref...  8.46 us
    all_gather x3, waiting for transfers between devices, one_layer(): lax.all_gather(tap_now, 'seqa', axis=0, tiled=True)  5.31 us
    dot_general x3, matrix products, one_layer(): jnp.dot(hidden, lax.all_gather(mixing, 'seqa', axis=1, tiled=True), prefe...  3.69 us
  transfers between devices with their start and end apart: 9, of which 6 were waited for; matrix products, arithmetic and copies ran while one was open for 13% of the time, Pallas kernels for 0%

commit v1 on v0

--- a/solution.py
+++ b/solution.py
@@ -7,6 +7,17 @@
 DILATION_FIRST1 = 128
 DILATION_SECOND2 = 512
 DILATION_THIRD3 = 2048
+
+
+def gather_around(x, axis, dim):
+    ways = lax.axis_size(axis)
+    pieces = [x]
+    for far in range(1, ways):
+        pieces.append(
+            lax.ppermute(pieces[far - 1], axis, [(d, (d - 1) % ways) for d in range(ways)])
+        )
+    line = jnp.concatenate(pieces, axis=dim)
+    return jnp.roll(line, lax.axis_index(axis) * x.shape[dim], axis=dim)
 
 
 def from_behind(value, axis, by):
@@ -41,9 +52,7 @@
     start_sum = jnp.broadcast_to(bias[None, :], (rows, bias.shape[0]))
     total = start_sum
     total = total + jnp.dot(
-        earlier,
-        lax.all_gather(tap_prev, "seqa", axis=0, tiled=True),
-        preferred_element_type=jnp.float32,
+        earlier, gather_around(tap_prev, "seqa", 0), preferred_element_type=jnp.float32
     )
     pre = total + jnp.dot(
         normed,

time: 174 us -> 151 us (0.87)
  the two profiles are of different devices: /device:TPU:0 before, /device:TPU:1 now
where the time goes in v1:
time: 151 us
  blocking collectives  47.2 us (31%)
  waiting for transfers between devices  34.1 us (23%)
  matrix products  30.6 us (20%)
  starting transfers between devices  20.6 us (14%)
  between operations  13.3 us (9%)
  local copies, waits for them, and re-layouts  4.5 us (3%)
    all_gather x3, blocking collectives, one_layer(): lax.all_gather(mixing, 'seqa', axis=1, tiled=True)  47.2 us
    ppermute x3, waiting for transfers between devices, from_behind(): return lax.ppermute(value, axis, pairs)  20.6 us
    dot_general x3, matrix products, one_layer(): jnp.dot(earlier, gather_around(tap_prev, 'seqa', 0), preferred_element_ty...  19.2 us
    ppermute x9, waiting for transfers between devices, gather_around(): lax.ppermute(pieces[far - 1], axis, [(d, (d - 1) % ways) for d in range(w...  12.8 us
    ppermute x3, starting transfers between devices, from_behind(): return lax.ppermute(value, axis, pairs)  10.6 us
    ppermute x9, starting transfers between devices, gather_around(): lax.ppermute(pieces[far - 1], axis, [(d, (d - 1) % ways) for d in range(w...  9.85 us
    dot_general x3, matrix products, one_layer(): jnp.dot(normed, lax.all_gather(tap_now, 'seqa', axis=0, tiled=True), pref...  7.84 us
    dot_general x3, matrix products, one_layer(): jnp.dot(hidden, lax.all_gather(mixing, 'seqa', axis=1, tiled=True), prefe...  3.64 us
  transfers between devices with their start and end apart: 15, of which 5 were waited for; matrix products, arithmetic and copies ran while one was open for 17% of the time, Pallas kernels for 0%

profile of v1, /device:TPU:1, one launch (start us, length us, event | category | flops | bytes accessed | tf_op | source)
XLA Modules:
  0.0 151.0 jit_solution(9808023765653381087)
XLA Ops:
  6.5 2.5 %fusion.75 = (bf16[1,160,1280]{2,1,0:T(8,128)(2,1)}, bf16[1,160,1280]{2,1,0:T(8,128)(2,1)}, bf16[1,160,1280]{2,1,0:T(8,128)(2,1)}) fusion(bf16[3,160,1280]{2,1,0:T(8,128)(2,1)} %param.9), kind=kLoop, calls=%fused_computation.114 | loop fusion | bytes 2457600 | tf_op jit(solution)/shard_map/slice | solution.py:78
  9.0 0.0 all-gather.10.cloned.1.call-update
  9.1 0.0 all-gather.12.cloned.1.call-start
  9.1 0.7 all-gather.12.cloned.1.call-update
  9.8 0.0 copy-start.3
  9.8 0.0 all-gather.14.cloned.1.call-start
  9.9 1.0 slice_bitcast_fusion
  10.9 0.0 collective-permute-start.1
  10.9 2.4 %collective-permute-start.5 = (bf16[160,1280]{1,0:T(8,128)(2,1)S(1)}, bf16[160,1280]{1,0:T(8,128)(2,1)}, u32[]{:S(2)}, u32[]{:S(2)}) collective-permute-start(bf16[160,1280]{1,0:T(8,128)(2,1)S(1)} %get-tuple-element.11), channel_id=1, source_target_pairs={{0,24},{8,0},{16,8},{24,16},{1,25},{9,1},{17,9},{25,17},{2,26},{10... | collective-permute-start | bytes 1228808 | tf_op jit(solution)/shard_map/ppermute | solution.py:17
  13.4 0.2 fusion.37
  13.6 0.0 copy-start.7
  13.6 0.2 fusion.38
  13.8 3.1 %collective-permute-start = (bf16[128,640]{1,0:T(8,128)(2,1)S(1)}, bf16[128,640]{1,0:T(8,128)(2,1)}, u32[]{:S(2)}, u32[]{:S(2)}) collective-permute-start(bf16[128,640]{1,0:T(8,128)(2,1)S(1)} %slice.80), channel_id=1, source_target_pairs={{0,1},{1,2},{2,3},{3,4},{4,5},{5,6},{6,7},{7,8},{8,9},{9,10},{10,1... | collective-permute-start | bytes 491528 | tf_op jit(solution)/shard_map/ppermute | solution.py:26
  16.9 1.6 %collective-permute-start.9 = (bf16[160,1280]{1,0:T(8,128)(2,1)}, bf16[160,1280]{1,0:T(8,128)(2,1)}, u32[]{:S(2)}, u32[]{:S(2)}) collective-permute-start(bf16[160,1280]{1,0:T(8,128)(2,1)} %get-tuple-element.9), channel_id=1, source_target_pairs={{0,24},{8,0},{16,8},{24,16},{1,25},{9,1},{17,9},{25,17},{2,26},{10... | collective-permute-start | bytes 1228808 | tf_op jit(solution)/shard_map/ppermute | solution.py:17
  18.5 0.0 all-gather.14.cloned.1.call-update
  18.6 0.9 collective-permute-done.1
  19.5 0.0 collective-permute-start.2
  19.5 0.1 fusion.76
  19.5 0.8 slice.81
  20.4 9.2 %collective-permute-done.5 = bf16[160,1280]{1,0:T(8,128)(2,1)} collective-permute-done((bf16[160,1280]{1,0:T(8,128)(2,1)S(1)}, bf16[160,1280]{1,0:T(8,128)(2,1)}, u32[]{:S(2)}, u32[]{:S(2)}) %collective-permute-start.5) | collective-permute-done | bytes 409632 | tf_op jit(solution)/shard_map/ppermute | solution.py:17
  29.6 1.6 %collective-permute-start.6 = (bf16[160,1280]{1,0:T(8,128)(2,1)}, bf16[160,1280]{1,0:T(8,128)(2,1)}, u32[]{:S(2)}, u32[]{:S(2)}) collective-permute-start(bf16[160,1280]{1,0:T(8,128)(2,1)} %collective-permute-done.5), channel_id=1, source_target_pairs={{0,24},{8,0},{16,8},{24,16},{1,25},{9,1},{17,9},{25,17},{2,26},{10... | collective-permute-start | bytes 1228808 | tf_op jit(solution)/shard_map/ppermute | solution.py:17
  31.2 26.3 %all-gather.1 = bf16[1,640,640]{1,2,0:T(8,128)(2,1)S(1)} all-gather(bf16[1,640,160]{1,2,0:T(8,128)(2,1)S(1)} %get-tuple-element.16), channel_id=3, replica_groups=mesh['seqa'=4,'seqb'=8] {'seqa'}, dimensions={2}, use_global_device_ids=true | all-gather | bytes 1024000 | tf_op jit(solution)/shard_map/all_gather | solution.py:65
  57.4 0.0 collective-permute-done.2
  57.4 0.5 collective-permute-start.3
  58.0 0.0 copy-start.4
  58.0 0.0 collective-permute-done.9
  58.0 3.4 %collective-permute-start.10 = (bf16[160,1280]{1,0:T(8,128)(2,1)}, bf16[160,1280]{1,0:T(8,128)(2,1)}, u32[]{:S(2)}, u32[]{:S(2)}) collective-permute-start(bf16[160,1280]{1,0:T(8,128)(2,1)} %collective-permute-done.9), channel_id=1, source_target_pairs={{0,24},{8,0},{16,8},{24,16},{1,25},{9,1},{17,9},{25,17},{2,26},{10... | collective-permute-start | bytes 1228808 | tf_op jit(solution)/shard_map/ppermute | solution.py:17
  61.4 0.0 collective-permute-done.6
  61.4 0.2 collective-permute-start.7
  61.6 2.6 %fusion.34 = f32[512,1280]{1,0:T(8,128)S(1)} fusion(bf16[512,640]{1,0:T(8,128)(2,1)S(1)} %fusion.38, bf16[1,640,1280]{2,1,0:T(8,128)(2,1)} %all-gather.10.cloned.1.call-done), kind=kOutput, calls=%fused_computation.58 | convolution fusion | flops 838860800 | bytes 4915200 | tf_op jit(solution)/shard_map/dot_general | solution.py:57
  64.2 2.7 %collective-permute-done.3 = bf16[160,1280]{1,0:T(8,128)(2,1)} collective-permute-done((bf16[160,1280]{1,0:T(8,128)(2,1)}, bf16[160,1280]{1,0:T(8,128)(2,1)}, u32[]{:S(2)}, u32[]{:S(2)}) %collective-permute-start.3) | collective-permute-done | bytes 409632 | tf_op jit(solution)/shard_map/ppermute | solution.py:17
  66.9 6.4 %fusion = f32[512,1280]{1,0:T(8,128)S(1)} fusion(f32[512,1280]{1,0:T(8,128)S(1)} %fusion.34, s32[]{:T(128)S(6)} %select_n.15, bf16[160,1280]{1,0:T(8,128)(2,1)} %get-tuple-element.10, bf16[160,1280]{1,0:T(8,128)(2,1)} %collective-permute-done.1, bf16[160,1280]{1,0:T(8,128)(2,1)} %collective-permute-done.2, bf16[160,1280]{1,0:T(8,128)(2,1)} %collective-permute-done.3, ...), kind=kOutput, calls=%fused_computation.3 | convolution fusion | flops 854589440 | bytes 7541764 | tf_op jit(solution)/shard_map/dot_general | solution.py:54
  73.3 1.0 multiply_reduce_fusion.1
  74.2 0.2 multiply_convert_fusion.1
  74.4 5.6 %collective-permute-start.4 = (bf16[512,640]{1,0:T(8,128)(2,1)S(1)}, bf16[512,640]{1,0:T(8,128)(2,1)S(1)}, u32[]{:S(2)}, u32[]{:S(2)}) collective-permute-start(bf16[512,640]{1,0:T(8,128)(2,1)S(1)} %multiply_convert_fusion.1), channel_id=1, source_target_pairs={{0,1},{1,2},{2,3},{3,4},{4,5},{5,6},{6,7},{7,8},{8,9},{9,10},{10,1... | collective-permute-start | bytes 1966088 | tf_op jit(solution)/shard_map/ppermute | solution.py:26
  80.0 10.6 %all-gather.3 = bf16[1,640,640]{1,2,0:T(8,128)(2,1)} all-gather(bf16[1,640,160]{1,2,0:T(8,128)(2,1)S(1)} %get-tuple-element.17), channel_id=5, replica_groups=mesh['seqa'=4,'seqb'=8] {'seqa'}, dimensions={2}, use_global_device_ids=true | all-gather | bytes 1024000 | tf_op jit(solution)/shard_map/all_gather | solution.py:65
  90.6 0.2 collective-permute-start.11
  90.7 2.6 %fusion.32 = f32[512,1280]{1,0:T(8,128)S(1)} fusion(bf16[512,640]{1,0:T(8,128)(2,1)S(1)} %multiply_convert_fusion.1, bf16[1,640,1280]{2,1,0:T(8,128)(2,1)} %all-gather.12.cloned.1.call-done), kind=kOutput, calls=%fused_computation.56 | convolution fusion | flops 838860800 | bytes 4915200 | tf_op jit(solution)/shard_map/dot_general | solution.py:57
  93.4 2.3 %collective-permute-done.4 = bf16[512,640]{1,0:T(8,128)(2,1)S(1)} collective-permute-done((bf16[512,640]{1,0:T(8,128)(2,1)S(1)}, bf16[512,640]{1,0:T(8,128)(2,1)S(1)}, u32[]{:S(2)}, u32[]{:S(2)}) %collective-permute-start.4) | collective-permute-done | bytes 655392 | tf_op jit(solution)/shard_map/ppermute | solution.py:26
  95.7 6.3 %fusion.1 = f32[512,1280]{1,0:T(8,128)S(1)} fusion(f32[512,1280]{1,0:T(8,128)S(1)} %fusion.32, bf16[512,640]{1,0:T(8,128)(2,1)S(1)} %collective-permute-done.4, s32[]{:T(128)S(6)} %select_n.15, bf16[160,1280]{1,0:T(8,128)(2,1)S(1)} %copy-done.6, bf16[160,1280]{1,0:T(8,128)(2,1)} %collective-permute-done.5, bf16[160,1280]{1,0:T(8,128)(2,1)} %collective-permute-done.6, ...), kind=kOutput, calls=%fused_computation.4 | convolution fusion | flops 853278720 | bytes 7541764 | tf_op jit(solution)/shard_map/dot_general | solution.py:54
  102.0 1.0 multiply_reduce_fusion
  102.9 0.2 multiply_convert_fusion
  103.1 1.9 %collective-permute-start.8 = (bf16[512,640]{1,0:T(8,128)(2,1)S(1)}, bf16[512,640]{1,0:T(8,128)(2,1)}, u32[]{:S(2)}, u32[]{:S(2)}) collective-permute-start(bf16[512,640]{1,0:T(8,128)(2,1)S(1)} %multiply_convert_fusion), channel_id=1, source_target_pairs={{0,4},{1,5},{2,6},{3,7},{4,8},{5,9},{6,10},{7,11},{8,12},{9,13},{1... | collective-permute-start | bytes 1966088 | tf_op jit(solution)/shard_map/ppermute | solution.py:26
  105.0 10.3 %all-gather.5 = bf16[1,640,640]{1,2,0:T(8,128)(2,1)S(1)} all-gather(bf16[1,640,160]{1,2,0:T(8,128)(2,1)S(1)} %get-tuple-element.15), channel_id=7, replica_groups=mesh['seqa'=4,'seqb'=8] {'seqa'}, dimensions={2}, use_global_device_ids=true | all-gather | bytes 1024000 | tf_op jit(solution)/shard_map/all_gather | solution.py:65
  115.3 2.6 %fusion.30 = f32[512,1280]{1,0:T(8,128)S(1)} fusion(bf16[512,640]{1,0:T(8,128)(2,1)S(1)} %multiply_convert_fusion, bf16[1,640,1280]{2,1,0:T(8,128)(2,1)} %all-gather.14.cloned.1.call-done), kind=kOutput, calls=%fused_computation.54 | convolution fusion | flops 838860800 | bytes 4915200 | tf_op jit(solution)/shard_map/dot_general | solution.py:57
  117.9 18.2 %collective-permute-done.8 = bf16[512,640]{1,0:T(8,128)(2,1)} collective-permute-done((bf16[512,640]{1,0:T(8,128)(2,1)S(1)}, bf16[512,640]{1,0:T(8,128)(2,1)}, u32[]{:S(2)}, u32[]{:S(2)}) %collective-permute-start.8) | collective-permute-done | bytes 655392 | tf_op jit(solution)/shard_map/ppermute | solution.py:26
  136.2 6.5 %fusion.2 = f32[512,1280]{1,0:T(8,128)S(1)} fusion(f32[512,1280]{1,0:T(8,128)S(1)} %fusion.30, bf16[512,640]{1,0:T(8,128)(2,1)} %collective-permute-done.8, s32[]{:T(128)S(6)} %select_n.15, bf16[160,1280]{1,0:T(8,128)(2,1)} %get-tuple-element.9, bf16[160,1280]{1,0:T(8,128)(2,1)} %collective-permute-done.9, bf16[160,1280]{1,0:T(8,128)(2,1)} %collective-permute-done.10, ...), kind=kOutput, calls=%fused_computation.5 | convolution fusion | flops 853278720 | bytes 7541764 | tf_op jit(solution)/shard_map/dot_general | solution.py:54
  142.7 1.7 %fusion.36 = bf16[512,640]{1,0:T(8,128)(2,1)} fusion(f32[512,640]{1,0:T(8,128)S(1)} %get-tuple-element.21, bf16[1,640,640]{1,2,0:T(8,128)(2,1)S(1)} %all-gather.5, f32[512,1280]{1,0:T(8,128)S(1)} %fusion.2), kind=kOutput, calls=%fused_computation.62 | convolution fusion | flops 421724160 | bytes 5406720 | tf_op jit(solution)/shard_map/dot_general | solution.py:63
  (26 shorter events, 0.1 us)
Async XLA Ops:
  6.5 3.3 %copy-start.1 = (bf16[3,160,1280]{2,1,0:T(8,128)(2,1)S(1)}, bf16[3,160,1280]{2,1,0:T(8,128)(2,1)}, u32[]{:S(2)}) copy-start(bf16[3,160,1280]{2,1,0:T(8,128)(2,1)} %param.8) | copy-start | bytes 3686404
  6.5 6.8 %copy-start = (bf16[512,640]{1,0:T(8,128)(2,1)S(1)}, bf16[512,640]{1,0:T(8,128)(2,1)}, u32[]{:S(2)}) copy-start(bf16[512,640]{1,0:T(8,128)(2,1)} %param.7) | copy-start | bytes 1966084
  6.5 55.0 %all-gather.10.cloned.1.call-start = ((), (), s32[]{:S(2)}) async-start(), calls=%async_computation | async-start | bytes 2048000 | tf_op jit(solution)/shard_map/all_gather | solution.py:59
  9.1 81.7 %all-gather.12.cloned.1.call-start = ((), (), s32[]{:S(2)}) async-start(), calls=%async_computation.1 | async-start | bytes 2048000 | tf_op jit(solution)/shard_map/all_gather | solution.py:59
  9.8 9.7 %copy-start.3 = (bf16[3,640,160]{1,2,0:T(8,128)(2,1)S(1)}, bf16[3,640,160]{1,2,0:T(8,128)(2,1)}, u32[]{:S(2)}) copy-start(bf16[3,640,160]{1,2,0:T(8,128)(2,1)} %param.11) | copy-start | bytes 1843204
  9.8 105.5 %all-gather.14.cloned.1.call-start = ((), (), s32[]{:S(2)}) async-start(), calls=%async_computation.2 | async-start | bytes 2048000 | tf_op jit(solution)/shard_map/all_gather | solution.py:59
  10.9 20.2 %copy-start.5 = (bf16[160,1280]{1,0:T(8,128)(2,1)}, bf16[160,1280]{1,0:T(8,128)(2,1)S(1)}, u32[]{:S(2)}) copy-start(bf16[160,1280]{1,0:T(8,128)(2,1)S(1)} %get-tuple-element.11) | copy-start | bytes 1228804
  10.9 8.5 %collective-permute-start.1 = (bf16[160,1280]{1,0:T(8,128)(2,1)}, bf16[160,1280]{1,0:T(8,128)(2,1)}, u32[]{:S(2)}, u32[]{:S(2)}) collective-permute-start(bf16[160,1280]{1,0:T(8,128)(2,1)} %get-tuple-element.10), channel_id=1, source_target_pairs={{0,24},{8,0},{16,8},{24,16},{1,25},{9,1},{17,9},{25,17},{2,26},{10... | collective-permute-start | bytes 1228808 | tf_op jit(solution)/shard_map/ppermute | solution.py:17
  10.9 18.6 %collective-permute-start.5 = (bf16[160,1280]{1,0:T(8,128)(2,1)S(1)}, bf16[160,1280]{1,0:T(8,128)(2,1)}, u32[]{:S(2)}, u32[]{:S(2)}) collective-permute-start(bf16[160,1280]{1,0:T(8,128)(2,1)S(1)} %get-tuple-element.11), channel_id=1, source_target_pairs={{0,24},{8,0},{16,8},{24,16},{1,25},{9,1},{17,9},{25,17},{2,26},{10... | collective-permute-start | bytes 1228808 | tf_op jit(solution)/shard_map/ppermute | solution.py:17
  13.6 44.4 %copy-start.7 = (f32[3,1280]{1,0:T(4,128)S(1)}, f32[3,1280]{1,0:T(4,128)}, u32[]{:S(2)}) copy-start(f32[3,1280]{1,0:T(4,128)} %param.10) | copy-start | bytes 46084
  13.8 50.4 %collective-permute-start = (bf16[128,640]{1,0:T(8,128)(2,1)S(1)}, bf16[128,640]{1,0:T(8,128)(2,1)}, u32[]{:S(2)}, u32[]{:S(2)}) collective-permute-start(bf16[128,640]{1,0:T(8,128)(2,1)S(1)} %slice.80), channel_id=1, source_target_pairs={{0,1},{1,2},{2,3},{3,4},{4,5},{5,6},{6,7},{7,8},{8,9},{9,10},{10,1... | collective-permute-start | bytes 491528 | tf_op jit(solution)/shard_map/ppermute | solution.py:26
  16.9 41.1 %collective-permute-start.9 = (bf16[160,1280]{1,0:T(8,128)(2,1)}, bf16[160,1280]{1,0:T(8,128)(2,1)}, u32[]{:S(2)}, u32[]{:S(2)}) collective-permute-start(bf16[160,1280]{1,0:T(8,128)(2,1)} %get-tuple-element.9), channel_id=1, source_target_pairs={{0,24},{8,0},{16,8},{24,16},{1,25},{9,1},{17,9},{25,17},{2,26},{10... | collective-permute-start | bytes 1228808 | tf_op jit(solution)/shard_map/ppermute | solution.py:17
  19.5 38.0 %collective-permute-start.2 = (bf16[160,1280]{1,0:T(8,128)(2,1)}, bf16[160,1280]{1,0:T(8,128)(2,1)}, u32[]{:S(2)}, u32[]{:S(2)}) collective-permute-start(bf16[160,1280]{1,0:T(8,128)(2,1)} %collective-permute-done.1), channel_id=1, source_target_pairs={{0,24},{8,0},{16,8},{24,16},{1,25},{9,1},{17,9},{25,17},{2,26},{10... | collective-permute-start | bytes 1228808 | tf_op jit(solution)/shard_map/ppermute | solution.py:17
  29.6 31.8 %collective-permute-start.6 = (bf16[160,1280]{1,0:T(8,128)(2,1)}, bf16[160,1280]{1,0:T(8,128)(2,1)}, u32[]{:S(2)}, u32[]{:S(2)}) collective-permute-start(bf16[160,1280]{1,0:T(8,128)(2,1)} %collective-permute-done.5), channel_id=1, source_target_pairs={{0,24},{8,0},{16,8},{24,16},{1,25},{9,1},{17,9},{25,17},{2,26},{10... | collective-permute-start | bytes 1228808 | tf_op jit(solution)/shard_map/ppermute | solution.py:17
  57.4 9.4 %collective-permute-start.3 = (bf16[160,1280]{1,0:T(8,128)(2,1)}, bf16[160,1280]{1,0:T(8,128)(2,1)}, u32[]{:S(2)}, u32[]{:S(2)}) collective-permute-start(bf16[160,1280]{1,0:T(8,128)(2,1)} %collective-permute-done.2), channel_id=1, source_target_pairs={{0,24},{8,0},{16,8},{24,16},{1,25},{9,1},{17,9},{25,17},{2,26},{10... | collective-permute-start | bytes 1228808 | tf_op jit(solution)/shard_map/ppermute | solution.py:17
  58.0 8.9 %copy-start.4 = (bf16[384,640]{1,0:T(8,128)(2,1)S(1)}, bf16[384,640]{1,0:T(8,128)(2,1)}, u32[]{:S(2)}) copy-start(bf16[384,640]{1,0:T(8,128)(2,1)} %slice.81) | copy-start | bytes 1474564
  58.0 32.6 %collective-permute-start.10 = (bf16[160,1280]{1,0:T(8,128)(2,1)}, bf16[160,1280]{1,0:T(8,128)(2,1)}, u32[]{:S(2)}, u32[]{:S(2)}) collective-permute-start(bf16[160,1280]{1,0:T(8,128)(2,1)} %collective-permute-done.9), channel_id=1, source_target_pairs={{0,24},{8,0},{16,8},{24,16},{1,25},{9,1},{17,9},{25,17},{2,26},{10... | collective-permute-start | bytes 1228808 | tf_op jit(solution)/shard_map/ppermute | solution.py:17
  61.4 32.0 %collective-permute-start.7 = (bf16[160,1280]{1,0:T(8,128)(2,1)}, bf16[160,1280]{1,0:T(8,128)(2,1)}, u32[]{:S(2)}, u32[]{:S(2)}) collective-permute-start(bf16[160,1280]{1,0:T(8,128)(2,1)} %collective-permute-done.6), channel_id=1, source_target_pairs={{0,24},{8,0},{16,8},{24,16},{1,25},{9,1},{17,9},{25,17},{2,26},{10... | collective-permute-start | bytes 1228808 | tf_op jit(solution)/shard_map/ppermute | solution.py:17
  74.4 21.3 %collective-permute-start.4 = (bf16[512,640]{1,0:T(8,128)(2,1)S(1)}, bf16[512,640]{1,0:T(8,128)(2,1)S(1)}, u32[]{:S(2)}, u32[]{:S(2)}) collective-permute-start(bf16[512,640]{1,0:T(8,128)(2,1)S(1)} %multiply_convert_fusion.1), channel_id=1, source_target_pairs={{0,1},{1,2},{2,3},{3,4},{4,5},{5,6},{6,7},{7,8},{8,9},{9,10},{10,1... | collective-permute-start | bytes 1966088 | tf_op jit(solution)/shard_map/ppermute | solution.py:26
  90.6 5.1 %copy-start.6 = (bf16[160,1280]{1,0:T(8,128)(2,1)S(1)}, bf16[160,1280]{1,0:T(8,128)(2,1)}, u32[]{:S(2)}) copy-start(bf16[160,1280]{1,0:T(8,128)(2,1)} %copy-done.5) | copy-start | bytes 1228804
  90.6 27.4 %collective-permute-start.11 = (bf16[160,1280]{1,0:T(8,128)(2,1)}, bf16[160,1280]{1,0:T(8,128)(2,1)}, u32[]{:S(2)}, u32[]{:S(2)}) collective-permute-start(bf16[160,1280]{1,0:T(8,128)(2,1)} %collective-permute-done.10), channel_id=1, source_target_pairs={{0,24},{8,0},{16,8},{24,16},{1,25},{9,1},{17,9},{25,17},{2,26},{10... | collective-permute-start | bytes 1228808 | tf_op jit(solution)/shard_map/ppermute | solution.py:17
  95.7 6.3 %copy-start.2 = (bf16[1,640,640]{1,2,0:T(8,128)(2,1)S(1)}, bf16[1,640,640]{1,2,0:T(8,128)(2,1)}, u32[]{:S(2)}) copy-start(bf16[1,640,640]{1,2,0:T(8,128)(2,1)} %all-gather.3) | copy-start | bytes 2457604
  103.1 33.1 %collective-permute-start.8 = (bf16[512,640]{1,0:T(8,128)(2,1)S(1)}, bf16[512,640]{1,0:T(8,128)(2,1)}, u32[]{:S(2)}, u32[]{:S(2)}) collective-permute-start(bf16[512,640]{1,0:T(8,128)(2,1)S(1)} %multiply_convert_fusion), channel_id=1, source_target_pairs={{0,4},{1,5},{2,6},{3,7},{4,8},{5,9},{6,10},{7,11},{8,12},{9,13},{1... | collective-permute-start | bytes 1966088 | tf_op jit(solution)/shard_map/ppermute | solution.py:26
Sparse Core Ops, SparseCore 0:
  9.2 26.9 all-gather.9
  37.7 22.9 all-gather.11
  62.3 24.6 all-gather.13
